TPU v7x, 512 devices: a whole 4x8x8 slice. The times are simulated.
512 devices in a mesh: blk: 64 (over x, y, core), spec: 8 (over z).
Axes of the slice: x: 4, y: 8, z: 8, core: 2. Of those that a mesh axis runs over, the one named last changes fastest.
Arguments:
- spectrum: float32 [32, 24, 65536], P('spec', None, 'blk'), may hold values from 0.05 to 2
- depths: float32 [65536], P('blk'), may hold values from 5 to 4000
- currents: float32 [2, 65536], P(None, 'blk'), may hold values from -4 to 4
- slopes: float32 [2, 65536], P(None, 'blk'), may hold values from -0.12 to 0.12
- wind_speed: float32 [2, 65536], P(None, 'blk'), may hold values from -40 to 40
- wet_mask: int32 [65536], P('blk'), may hold values 0 or 1
- face_owner: int32 [4096, 1], P('blk'), may hold values from 0 to 63, as said below
- face_block: int32 [4096], P('blk'), may hold values from 0 to 15
- freq_weights: bfloat16 [2, 32, 32], replicated, may hold values from 0.0049743652 to 0.079589844
- angle_weights: bfloat16 [2, 2, 24, 24], replicated, may hold values from 0.0049743652 to 0.099609375
- transfer_rate: float32 [32], replicated, may hold values from 0.05 to 0.3
Outputs:
- next_spectrum: float32 [32, 24, 65536], P('spec', None, 'blk')
Inputs may be any that keep to these rules, and one draw needn't show every extreme that they name: `face_owner`: face i of one device is side i % 4 (west, east, south, north) of its block i // 4. Of the 64 rows of one device, 32 name another index and the rest name the device itself; no other index is named more than 2 times in those rows, and one is named exactly 2 times.
All inputs are finite; a program needn't handle non-finite values. No bound on the sum of `wet_mask` on one device may be relied on, other than what follows from the above.
Results may differ from a plain program's by a relative error of at most 0.0011.
The roundings to bfloat16 on the way count: a program that leaves them out, or rounds other values in their place, can miss the bound.
Values may be sent and summed in bfloat16 or wider, within the bound.
A program may use at most 64 MiB of HBM per device.

v0:
```python
import math
import jax
import jax.numpy as jnp
from jax import lax
from jax.sharding import PartitionSpec as P

TILE = 8
GRAVITY = 9.81
TIME_STEP = 200.0
CELL_SIZE = 5500.0
LOWEST_FREQ = 0.0418
FREQ_GROWTH = 1.1
WIND_GROWTH = 0.0003
TURN_LIMIT = 0.9


def dispersion(radian_freq, water_depth):
    deep_kh = radian_freq * radian_freq / GRAVITY * water_depth
    wave_kh = deep_kh / jnp.sqrt(jnp.tanh(deep_kh))
    decay_two = jnp.exp(-2.0 * wave_kh)
    denom_term = 1.0 - decay_two * decay_two
    shoal_ratio = 4.0 * wave_kh * decay_two / denom_term
    phase_speed = radian_freq * water_depth / wave_kh
    group_speed = 0.5 * (1.0 + shoal_ratio) * phase_speed
    turn_factor = 2.0 * radian_freq * decay_two / denom_term
    return (phase_speed, group_speed, turn_factor)


def courants(radian_freq, angle_values, water_depth, current_xy, slope_xy, wet_float):
    freq_column = radian_freq[:, None, None, None, None]
    phase_speed, group_speed, turn_factor = dispersion(freq_column, water_depth[None, None])
    cosine = jnp.cos(angle_values)[None, :, None, None, None]
    sine = jnp.sin(angle_values)[None, :, None, None, None]
    grid_ratio = TIME_STEP / CELL_SIZE
    cour_x = (group_speed * cosine + current_xy[0][None, None]) * grid_ratio * wet_float[None, None]
    cour_y = (group_speed * sine + current_xy[1][None, None]) * grid_ratio * wet_float[None, None]
    angle_step = 2.0 * math.pi / angle_values.shape[0]
    turning = (
        turn_factor
        * (sine * slope_xy[0][None, None] - cosine * slope_xy[1][None, None])
        * (TIME_STEP / angle_step)
    )
    cour_turn = jnp.clip(turning, -TURN_LIMIT, TURN_LIMIT)
    return (phase_speed, cour_x, cour_y, cour_turn)


def edge_fluxes(wave_field, cour_x, cour_y):
    west_side = jnp.maximum(-cour_x[..., :, 0], 0.0) * wave_field[..., :, 0]
    east_side = jnp.maximum(cour_x[..., :, -1], 0.0) * wave_field[..., :, -1]
    south_side = jnp.maximum(-cour_y[..., 0, :], 0.0) * wave_field[..., 0, :]
    north_side = jnp.maximum(cour_y[..., -1, :], 0.0) * wave_field[..., -1, :]
    return jnp.stack([west_side, east_side, south_side, north_side], axis=3)


def transported(wave_field, cour_x, cour_y, cour_turn, inflow):
    tile_side = wave_field.shape[-1]
    rightward = jnp.maximum(cour_x, 0.0) * wave_field
    leftward = jnp.maximum(-cour_x, 0.0) * wave_field
    upward = jnp.maximum(cour_y, 0.0) * wave_field
    downward = jnp.maximum(-cour_y, 0.0) * wave_field
    lead_pads = [(0, 0)] * 3
    from_x = jnp.pad(rightward[..., :, :-1], lead_pads + [(0, 0), (1, 0)]) + jnp.pad(
        leftward[..., :, 1:], lead_pads + [(0, 0), (0, 1)]
    )
    from_y = jnp.pad(upward[..., :-1, :], lead_pads + [(1, 0), (0, 0)]) + jnp.pad(
        downward[..., 1:, :], lead_pads + [(0, 1), (0, 0)]
    )
    from_turn = jnp.roll(jnp.maximum(cour_turn, 0.0) * wave_field, 1, axis=1) + jnp.roll(
        jnp.maximum(-cour_turn, 0.0) * wave_field, -1, axis=1
    )
    ghost_x = jnp.pad(inflow[:, :, :, 0, :, None], lead_pads + [(0, 0), (0, tile_side - 1)])
    ghost_x = ghost_x + jnp.pad(
        inflow[:, :, :, 1, :, None], lead_pads + [(0, 0), (tile_side - 1, 0)]
    )
    ghost_y = jnp.pad(inflow[:, :, :, 2, None, :], lead_pads + [(0, tile_side - 1), (0, 0)])
    ghost_y = ghost_y + jnp.pad(
        inflow[:, :, :, 3, None, :], lead_pads + [(tile_side - 1, 0), (0, 0)]
    )
    outflow = (jnp.abs(cour_x) + jnp.abs(cour_y) + jnp.abs(cour_turn)) * wave_field
    return wave_field - outflow + from_x + from_y + from_turn + ghost_x + ghost_y


def nonlinear(levels, freq_weights, angle_weights, transfer_rate):
    levels_wide = levels.astype(jnp.float32)
    shifted_plus = jnp.einsum(
        "gf,fdq->gdq", freq_weights[0], levels, preferred_element_type=jnp.float32
    ).astype(jnp.bfloat16)
    shifted_minus = jnp.einsum(
        "gf,fdq->gdq", freq_weights[1], levels, preferred_element_type=jnp.float32
    ).astype(jnp.bfloat16)
    rate_column = transfer_rate[:, None, None]
    delta_list = []
    for mirror in range(2):
        image_plus = jnp.einsum(
            "ed,gdq->geq",
            angle_weights[mirror, 0],
            shifted_plus,
            preferred_element_type=jnp.float32,
        )
        image_minus = jnp.einsum(
            "ed,gdq->geq",
            angle_weights[mirror, 1],
            shifted_minus,
            preferred_element_type=jnp.float32,
        )
        delta_list.append(
            rate_column
            * (
                levels_wide * levels_wide * (image_plus + image_minus)
                - 2.0 * levels_wide * image_plus * image_minus
            )
        )
    low_first = delta_list[0].astype(jnp.bfloat16)
    low_second = delta_list[1].astype(jnp.bfloat16)
    back_plus = (
        jnp.einsum(
            "ed,geq->gdq", angle_weights[0, 0], low_first, preferred_element_type=jnp.float32
        )
        + jnp.einsum(
            "ed,geq->gdq", angle_weights[1, 0], low_second, preferred_element_type=jnp.float32
        )
    ).astype(jnp.bfloat16)
    back_minus = (
        jnp.einsum(
            "ed,geq->gdq", angle_weights[0, 1], low_first, preferred_element_type=jnp.float32
        )
        + jnp.einsum(
            "ed,geq->gdq", angle_weights[1, 1], low_second, preferred_element_type=jnp.float32
        )
    ).astype(jnp.bfloat16)
    spread_plus = jnp.einsum(
        "gf,gdq->fdq", freq_weights[0], back_plus, preferred_element_type=jnp.float32
    )
    spread_minus = jnp.einsum(
        "gf,gdq->fdq", freq_weights[1], back_minus, preferred_element_type=jnp.float32
    )
    return -2.0 * (delta_list[0] + delta_list[1]) + spread_plus + spread_minus


def shards(
    spectrum,
    depths,
    currents,
    slopes,
    wind_speed,
    wet_mask,
    face_owner,
    face_block,
    freq_weights,
    angle_weights,
    transfer_rate,
):
    freq_local, angle_count, point_count = spectrum.shape
    block_count = point_count // (TILE * TILE)
    group_count = lax.axis_size("spec")
    peer_count = lax.axis_size("blk")
    my_index = lax.axis_index("blk")
    face_count = face_block.shape[0]
    remote_total = face_count // 2
    capacity = max(2, (remote_total + peer_count - 2) // (peer_count - 1))
    first_freq = lax.axis_index("spec") * freq_local
    freq_index = (first_freq + jnp.arange(freq_local, dtype=jnp.int32)).astype(jnp.float32)
    radian_freq = 2.0 * math.pi * LOWEST_FREQ * jnp.power(jnp.float32(FREQ_GROWTH), freq_index)
    angle_values = jnp.arange(angle_count, dtype=jnp.int32).astype(jnp.float32) * (
        2.0 * math.pi / angle_count
    )
    wet_float = wet_mask.astype(jnp.float32)
    wave_field = spectrum.reshape(freq_local, angle_count, block_count, TILE, TILE)
    phase_speed, cour_x, cour_y, cour_turn = courants(
        radian_freq,
        angle_values,
        depths.reshape(block_count, TILE, TILE),
        currents.reshape(2, block_count, TILE, TILE),
        slopes.reshape(2, block_count, TILE, TILE),
        wet_float.reshape(block_count, TILE, TILE),
    )
    edges = edge_fluxes(wave_field, cour_x, cour_y)
    edge_rows = edges.transpose(2, 3, 0, 1, 4).reshape(
        block_count * 4, freq_local * angle_count * TILE
    )
    owners = face_owner[:, 0]
    face_sides = jnp.arange(face_count, dtype=jnp.int32) % 4
    wanted_ids = face_block * 4 + jnp.bitwise_xor(face_sides, 1)
    remote_face = (owners != my_index).astype(jnp.int32)
    peer_onehot = (owners[:, None] == jnp.arange(peer_count, dtype=jnp.int32)[None, :]).astype(
        jnp.int32
    ) * remote_face[:, None]
    earlier = jnp.cumsum(peer_onehot, axis=0) - peer_onehot
    slot_ranks = jnp.sum(earlier * peer_onehot, axis=1)
    slot_range = jnp.arange(capacity, dtype=jnp.int32)
    slot_onehot = (slot_ranks[:, None] == slot_range[None, :]).astype(jnp.int32)
    requests = jnp.sum(
        peer_onehot[:, :, None] * (slot_onehot * wanted_ids[:, None])[:, None, :], axis=0
    )
    located = jnp.take(
        edge_rows, lax.all_to_all(requests, "blk", split_axis=0, concat_axis=0, tiled=True), axis=0
    )
    replies = lax.all_to_all(located, "blk", split_axis=0, concat_axis=0, tiled=True)
    remote_index = jnp.where(remote_face > 0, owners * capacity + slot_ranks, 0)
    remote_rows = jnp.take(replies.reshape(peer_count * capacity, -1), remote_index, axis=0)
    local_rows = jnp.take(edge_rows, wanted_ids, axis=0)
    inflow_rows = jnp.where(remote_face[:, None] > 0, remote_rows, local_rows)
    inflow = inflow_rows.reshape(block_count, 4, freq_local, angle_count, TILE).transpose(
        2, 3, 0, 1, 4
    )
    moved = transported(wave_field, cour_x, cour_y, cour_turn, inflow).reshape(
        freq_local, angle_count, point_count
    )
    levels = moved.astype(jnp.bfloat16).reshape(
        freq_local, angle_count, group_count, point_count // group_count
    )
    result = nonlinear(
        lax.all_to_all(levels, "spec", split_axis=2, concat_axis=0, tiled=True)[:, :, 0, :],
        freq_weights,
        angle_weights,
        transfer_rate,
    )
    item_width = result.shape[2]
    split_rows = result.reshape(group_count, freq_local, angle_count, item_width)
    returned = lax.all_to_all(split_rows, "spec", split_axis=0, concat_axis=0, tiled=True)
    transfer = returned.transpose(1, 2, 0, 3).reshape(freq_local, angle_count, point_count)
    along_wind = (
        wind_speed[0][None, None, :] * jnp.cos(angle_values)[None, :, None]
        + wind_speed[1][None, None, :] * jnp.sin(angle_values)[None, :, None]
    )
    phase_flat = phase_speed.reshape(freq_local, 1, point_count)
    growth = (
        TIME_STEP
        * WIND_GROWTH
        * radian_freq[:, None, None]
        * jnp.maximum(along_wind / phase_flat - 1.0, 0.0)
    )
    return wet_float[None, None, :] * (moved + transfer + growth * moved)


def solution(mesh):
    in_specs = (
        P("spec", None, "blk"),
        P("blk"),
        P(None, "blk"),
        P(None, "blk"),
        P(None, "blk"),
        P("blk"),
        P("blk", None),
        P("blk"),
        P(),
        P(),
        P(),
    )
    out_specs = P("spec", None, "blk")
    return jax.shard_map(shards, mesh=mesh, in_specs=in_specs, out_specs=out_specs, check_vma=False)
```

profile of v0, /device:TPU:6, one launch (start us, length us, event | category | flops | bytes accessed | tf_op | source)
XLA Modules:
  0.0 151.9 jit_solution(5503527234569175041)
XLA Ops:
  0.0 1.2 compare_reduce_fusion
  2.9 1.2 compare_and_fusion
  4.9 11.0 %all-to-all-start = ((s32[64,1,2]{2,1,0:T(1,128)}), s32[64,1,2]{2,1,0:T(1,128)}, u32[]{:S(2)}, u32[]{:S(2)}) async-start(s32[64,1,2]{2,1,0:T(1,128)} %copy.142), calls=%async_computation | async-start | bytes 65536 | tf_op jit(solution)/shard_map/all_to_all | solution.py:196
  20.3 1.6 %copy.138 = f32[4,24,1024]{1,2,0:T(8,128)S(1)} copy(f32[4,24,1024]{2,1,0:T(8,128)} %param.11) | data formatting | bytes 786432 | tf_op args[0]
  23.0 1.4 copy-done
  24.4 1.3 slice_multiply_fusion.7
  28.8 1.2 multiply_subtract_fusion.1
  30.0 2.4 %maximum_multiply_fusion.1 = (f32[4,24,16,8,8]{1,4,3,2,0:T(8,128)}, f32[4,24,16,8,8]{1,4,3,2,0:T(8,128)}) fusion(f32[4,24,16,8,8]{1,4,3,2,0:T(8,128)S(1)} %bitcast.143, f32[24,16,8,8]{0,3,2,1:T(8,128)S(1)} %multiply_subtract_fusion.1, f32[4,16,8,8]{3,2,1,0:T(8,128)S(1)} %copy.141), kind=kLoop, calls=%fused_computation.17 | loop fusion | flops 786432 | bytes 1294336 | tf_op jit(solution)/shard_map/mul | solution.py:68
  32.5 1.1 maximum_bitcast_fusion
  33.6 3.2 %copy.145 = f32[16,4,4,24,8]{4,3,2,1,0:T(8,128)} copy(f32[16,4,4,24,8]{3,4,1,0,2:T(8,128)} %maximum_bitcast_fusion) | data formatting | bytes 393216 | tf_op jit(solution)/shard_map/transpose | solution.py:178
  36.8 3.4 %reshape.422 = f32[64,768]{1,0:T(8,128)S(1)} reshape(f32[16,4,4,24,8]{4,3,2,1,0:T(8,128)} %copy.145) | data formatting | bytes 393216 | tf_op jit(solution)/shard_map/reshape | solution.py:178
  40.9 3.4 %gather.20 = f32[16,4,4,24,8]{4,3,2,1,0:T(8,128)} reshape(f32[64,768]{1,0:T(8,128)S(1)} %gather_fusion.2) | data formatting | bytes 393216 | tf_op jit(solution)/shard_map/jit(_take)/gather | solution.py:201
  44.2 3.2 %copy.149 = f32[16,4,4,24,8]{3,4,1,0,2:T(8,128)} copy(f32[16,4,4,24,8]{4,3,2,1,0:T(8,128)} %gather.20) | data formatting | bytes 393216 | tf_op jit(solution)/shard_map/jit(_take)/gather | solution.py:201
  48.3 3.7 %slice.162 = f32[4,1,16,8,8]{1,4,3,2,0:T(8,128)} slice(f32[4,24,16,8,8]{1,4,3,2,0:T(8,128)} %get-tuple-element.23), slice={[0:4], [23:24], [0:16], [0:8], [0:8]} | slice | bytes 32768 | tf_op jit(solution)/shard_map/jit(_roll_static)/slice | solution.py:68
  51.9 2.0 %slice.164 = f32[4,23,16,8,8]{1,4,3,2,0:T(8,128)} slice(f32[4,24,16,8,8]{1,4,3,2,0:T(8,128)S(1)} %copy-done.3), slice={[0:4], [1:24], [0:16], [0:8], [0:8]} | slice | bytes 753664 | tf_op jit(solution)/shard_map/jit(_roll_static)/slice | solution.py:68
  55.6 1.6 %gather_fusion = f32[128,768]{1,0:T(8,128)} fusion(f32[64,768]{1,0:T(8,128)S(1)} %reshape.422, s32[1024]{0:T(1024)S(1)} %pad_clamp_fusion.2), kind=kCustom, calls=%fused_computation | custom fusion | bytes 786944 | tf_op jit(solution)/shard_map/jit(_take)/gather | solution.py:195
  57.1 1.2 reshape.428
  60.0 10.5 %all-to-all-start.1 = ((f32[64,2,768]{2,1,0:T(2,128)}), f32[64,2,768]{2,1,0:T(2,128)}, u32[]{:S(2)}, u32[]{:S(2)}) async-start(f32[64,2,768]{2,1,0:T(2,128)} %broadcast_select_fusion), calls=%async_computation.1 | async-start | bytes 786432 | tf_op jit(solution)/shard_map/all_to_all | solution.py:198
  70.5 4.4 %slice_multiply_fusion.3 = (f32[4,24,16,7,8]{1,4,3,2,0:T(8,128)}, f32[4,24,16,7,8]{1,4,3,2,0:T(8,128)}) fusion(f32[4,24,16,8,8]{1,4,3,2,0:T(8,128)S(1)} %bitcast.144, f32[4,24,16,8,8]{1,4,3,2,0:T(8,128)} %copy-done.5), kind=kLoop, calls=%fused_computation.24 | loop fusion | flops 430080 | bytes 2064384 | tf_op jit(solution)/shard_map/mul | solution.py:59
  75.0 2.6 %slice_multiply_fusion.1 = (f32[4,24,16,8,7]{1,4,3,2,0:T(8,128)}, f32[4,24,16,8,7]{1,4,3,2,0:T(8,128)}) fusion(f32[4,24,16,8,8]{1,4,3,2,0:T(8,128)S(1)} %bitcast.145, f32[4,24,16,8,8]{1,4,3,2,0:T(8,128)S(1)} %copy-done.1), kind=kLoop, calls=%fused_computation.12 | loop fusion | flops 430080 | bytes 2064384 | tf_op jit(solution)/shard_map/mul | solution.py:57
  77.6 7.0 %all-to-all-done.1 = f32[64,2,768]{2,1,0:T(2,128)} async-done(((f32[64,2,768]{2,1,0:T(2,128)}), f32[64,2,768]{2,1,0:T(2,128)}, u32[]{:S(2)}, u32[]{:S(2)}) %all-to-all-start.1) | async-done | bytes 393248 | tf_op jit(solution)/shard_map/all_to_all | solution.py:198
  84.6 1.3 reshape.423
  85.9 1.5 gather_fusion.1
  87.3 3.8 %gather.18 = f32[16,4,4,24,8]{4,3,2,1,0:T(8,128)} reshape(f32[64,768]{1,0:T(8,128)} %gather_fusion.1) | data formatting | bytes 393216 | tf_op jit(solution)/shard_map/jit(_take)/gather | solution.py:200
  91.2 3.2 %copy.148 = f32[16,4,4,24,8]{3,4,1,0,2:T(8,128)} copy(f32[16,4,4,24,8]{4,3,2,1,0:T(8,128)} %gather.18) | data formatting | bytes 393216 | tf_op jit(solution)/shard_map/jit(_take)/gather | solution.py:200
  94.3 2.0 %select_bitcast_fusion = f32[4,24,16,4,8]{1,4,3,2,0:T(8,128)S(1)} fusion(f32[16,4,4,24,8]{3,4,1,0,2:T(8,128)} %copy.149, f32[16,4,4,24,8]{3,4,1,0,2:T(8,128)} %copy.148, pred[16,4]{1,0:T(8,128)(4,1)S(1)} %copy-done.28, pred[16,4]{1,0:T(8,128)(4,1)S(1)} %broadcast_in_dim.64, pred[16,4]{1,0:T(8,128)(4,1)S(1)} %broadcast_in_dim.62), kind=kLoop, calls=%fused_computation.41 | loop fusion | flops 147456 | bytes 590016 | tf_op jit(solution)/shard_map/transpose | solution.py:203
  96.8 1.2 copy-done.2
  98.7 7.7 %fusion.97 = (bf16[4,24,16,8,8]{1,4,3,2,0:T(8,128)(2,1)}, f32[4,24,16,8,8]{1,4,3,2,0:T(8,128)}) fusion(f32[4,24,16,1,8]{1,4,3,2,0:T(8,128)S(1)} %get-tuple-element.26, f32[4,24,16,1,8]{1,4,3,2,0:T(8,128)S(1)} %get-tuple-element.27, f32[4,24,16,8,8]{1,3,2,0,4:T(8,128)S(1)} %pad_add_fusion, f32[4,1,16,8,8]{1,4,3,2,0:T(8,128)S(1)} %bitcast.148, ...), kind=kLoop, calls=%fused_computation.176 | loop fusion | flops 2752512 | bytes 3780800 | tf_op jit(solution)/shard_map/convert_element_type | solution.py:209
  106.3 1.6 %copy.152 = bf16[4,24,8,128]{3,1,0,2:T(8,128)(2,1)S(1)} copy(bf16[4,24,8,128]{1,3,2,0:T(8,128)(2,1)} %bitcast.154) | data formatting | bytes 393216 | tf_op jit(solution)/shard_map/convert_element_type | solution.py:209
  107.9 21.1 %all_to_all.40 = bf16[4,24,8,128]{3,1,0,2:T(8,128)(2,1)S(1)} all-to-all(bf16[4,24,8,128]{3,1,0,2:T(8,128)(2,1)S(1)} %copy.152), channel_id=1, replica_groups=mesh['blk'=64,'spec'=8] {'spec'}, dimensions={2} | all-to-all | bytes 393216 | tf_op jit(solution)/shard_map/all_to_all | solution.py:213
  133.3 3.5 %all-to-all-start.3 = ((f32[8,4,24,128]{3,1,2,0:T(4,128)}), f32[8,4,24,128]{3,1,2,0:T(4,128)S(1)}, u32[]{:S(2)}, u32[]{:S(2)}) async-start(f32[8,4,24,128]{3,1,2,0:T(4,128)} %copy.174), calls=%async_computation.3 | async-start | bytes 786432 | tf_op jit(solution)/shard_map/all_to_all | solution.py:220
  137.6 13.1 %all-to-all-done.3 = f32[8,4,24,128]{3,1,2,0:T(4,128)S(1)} async-done(((f32[8,4,24,128]{3,1,2,0:T(4,128)}), f32[8,4,24,128]{3,1,2,0:T(4,128)S(1)}, u32[]{:S(2)}, u32[]{:S(2)}) %all-to-all-start.3) | async-done | bytes 393248 | tf_op jit(solution)/shard_map/all_to_all | solution.py:220
  (138 shorter events, 22.6 us)
Async XLA Ops:
  4.9 49.0 %all-to-all-start = ((s32[64,1,2]{2,1,0:T(1,128)}), s32[64,1,2]{2,1,0:T(1,128)}, u32[]{:S(2)}, u32[]{:S(2)}) async-start(s32[64,1,2]{2,1,0:T(1,128)} %copy.142), calls=%async_computation | async-start | bytes 65536 | tf_op jit(solution)/shard_map/all_to_all | solution.py:196
  15.9 7.0 %copy-start.29 = (f32[4]{0:T(128)}, f32[4]{0:T(128)S(1)}, u32[]{:S(2)}) copy-start(f32[4]{0:T(128)S(1)} %get-tuple-element.41) | copy-start | bytes 52
  16.0 7.0 %copy-start.31 = (f32[4]{0:T(128)}, f32[4]{0:T(128)S(1)}, u32[]{:S(2)}) copy-start(f32[4]{0:T(128)S(1)} %broadcast_multiply_fusion.3) | copy-start | bytes 52
  16.0 12.7 %copy-start.21 = (f32[24]{0:T(128)}, f32[24]{0:T(128)S(1)}, u32[]{:S(2)}) copy-start(f32[24]{0:T(128)S(1)} %get-tuple-element.43) | copy-start | bytes 292
  16.0 12.7 %copy-start.24 = (f32[24]{0:T(128)}, f32[24]{0:T(128)S(1)}, u32[]{:S(2)}) copy-start(f32[24]{0:T(128)S(1)} %get-tuple-element.44) | copy-start | bytes 292
  19.3 3.6 %copy-start.11 = (f32[16,8,8]{2,1,0:T(8,128)}, f32[16,8,8]{2,1,0:T(8,128)S(1)}, u32[]{:S(2)}) copy-start(f32[16,8,8]{2,1,0:T(8,128)S(1)} %add.194) | copy-start | bytes 12292
  19.4 3.5 %copy-start.13 = (f32[16,8,8]{2,1,0:T(8,128)}, f32[16,8,8]{2,1,0:T(8,128)S(1)}, u32[]{:S(2)}) copy-start(f32[16,8,8]{2,1,0:T(8,128)S(1)} %add.197) | copy-start | bytes 12292
  20.3 2.7 %copy-start.15 = (f32[16,8,8]{2,1,0:T(8,128)}, f32[16,8,8]{2,1,0:T(8,128)S(1)}, u32[]{:S(2)}) copy-start(f32[16,8,8]{2,1,0:T(8,128)S(1)} %mul.536) | copy-start | bytes 12292
  23.0 2.7 %copy-start.5 = (f32[4,24,16,8,8]{1,4,3,2,0:T(8,128)}, f32[4,24,16,8,8]{1,4,3,2,0:T(8,128)S(1)}, u32[]{:S(2)}) copy-start(f32[4,24,16,8,8]{1,4,3,2,0:T(8,128)S(1)} %get-tuple-element.30) | copy-start | bytes 1179652
  30.0 2.5 %copy-start.8 = (f32[4,24,16,8,1]{1,4,3,2,0:T(1,128)S(1)}, f32[4,24,16,8,1]{1,4,3,2,0:T(1,128)}, u32[]{:S(2)}) copy-start(f32[4,24,16,8,1]{1,4,3,2,0:T(1,128)} %get-tuple-element.20) | copy-start | bytes 147460
  30.0 2.5 %copy-start.9 = (f32[4,24,16,1,8]{1,4,3,2,0:T(8,128)S(1)}, f32[4,24,16,1,8]{1,4,3,2,0:T(8,128)}, u32[]{:S(2)}) copy-start(f32[4,24,16,1,8]{1,4,3,2,0:T(8,128)} %get-tuple-element.21) | copy-start | bytes 147460
  30.0 2.5 %copy-start.10 = (f32[4,24,16,1,8]{1,4,3,2,0:T(8,128)S(1)}, f32[4,24,16,1,8]{1,4,3,2,0:T(8,128)}, u32[]{:S(2)}) copy-start(f32[4,24,16,1,8]{1,4,3,2,0:T(8,128)} %get-tuple-element.22) | copy-start | bytes 147460
  44.2 3.3 %copy-start.33 = (pred[64]{0:T(512)(128)(4,1)S(1)}, pred[64]{0:T(512)(128)(4,1)}, u32[]{:S(2)}) copy-start(pred[64]{0:T(512)(128)(4,1)} %get-tuple-element.37) | copy-start | bytes 196
  44.2 3.4 %copy-start.35 = (pred[64]{0:T(512)(128)(4,1)S(1)}, pred[64]{0:T(512)(128)(4,1)}, u32[]{:S(2)}) copy-start(pred[64]{0:T(512)(128)(4,1)} %get-tuple-element.13) | copy-start | bytes 196
  48.3 3.7 %copy-start.3 = (f32[4,24,16,8,8]{1,4,3,2,0:T(8,128)S(1)}, f32[4,24,16,8,8]{1,4,3,2,0:T(8,128)}, u32[]{:S(2)}) copy-start(f32[4,24,16,8,8]{1,4,3,2,0:T(8,128)} %get-tuple-element.24) | copy-start | bytes 1179652
  60.0 24.6 %all-to-all-start.1 = ((f32[64,2,768]{2,1,0:T(2,128)}), f32[64,2,768]{2,1,0:T(2,128)}, u32[]{:S(2)}, u32[]{:S(2)}) async-start(f32[64,2,768]{2,1,0:T(2,128)} %broadcast_select_fusion), calls=%async_computation.1 | async-start | bytes 786432 | tf_op jit(solution)/shard_map/all_to_all | solution.py:198
  70.5 4.4 %copy-start.1 = (f32[4,24,16,8,8]{1,4,3,2,0:T(8,128)S(1)}, f32[4,24,16,8,8]{1,4,3,2,0:T(8,128)}, u32[]{:S(2)}) copy-start(f32[4,24,16,8,8]{1,4,3,2,0:T(8,128)} %copy-done) | copy-start | bytes 1179652
  91.2 3.2 %copy-start.28 = (pred[16,4]{1,0:T(8,128)(4,1)S(1)}, pred[16,4]{1,0:T(8,128)(4,1)}, u32[]{:S(2)}) copy-start(pred[16,4]{1,0:T(8,128)(4,1)} %broadcast_in_dim.69) | copy-start | bytes 196
  94.3 2.4 %copy-start.6 = (f32[4,1,16,8,8]{1,4,3,2,0:T(8,128)S(1)}, f32[4,1,16,8,8]{1,4,3,2,0:T(8,128)}, u32[]{:S(2)}) copy-start(f32[4,1,16,8,8]{1,4,3,2,0:T(8,128)} %slice.162) | copy-start | bytes 49156
  96.4 2.3 %copy-start.4 = (f32[4,24,16,8,8]{1,4,3,2,0:T(8,128)S(1)}, f32[4,24,16,8,8]{1,4,3,2,0:T(8,128)}, u32[]{:S(2)}) copy-start(f32[4,24,16,8,8]{1,4,3,2,0:T(8,128)} %get-tuple-element.24) | copy-start | bytes 1179652
  98.6 30.5 %copy-start.18 = (bf16[2,32,32]{2,1,0:T(8,128)(2,1)S(1)}, bf16[2,32,32]{2,1,0:T(8,128)(2,1)}, u32[]{:S(2)}) copy-start(bf16[2,32,32]{2,1,0:T(8,128)(2,1)} %param.19) | copy-start | bytes 12292
  106.3 23.0 %copy-start.17 = (bf16[2,2,24,24]{3,2,1,0:T(8,128)(2,1)S(1)}, bf16[2,2,24,24]{3,2,1,0:T(8,128)(2,1)}, u32[]{:S(2)}) copy-start(bf16[2,2,24,24]{3,2,1,0:T(8,128)(2,1)} %param.20) | copy-start | bytes 13828
  107.9 22.4 %copy-start.34 = (f32[32]{0:T(128)S(1)}, f32[32]{0:T(128)}, u32[]{:S(2)}) copy-start(f32[32]{0:T(128)} %param.21) | copy-start | bytes 388
  131.7 5.1 %copy-start.19 = (s32[1024]{0:T(1024)S(1)}, s32[1024]{0:T(1024)}, u32[]{:S(2)}) copy-start(s32[1024]{0:T(1024)} %param.16) | copy-start | bytes 12292
  131.7 5.1 %copy-start.27 = (f32[2,1024]{1,0:T(2,128)S(1)}, f32[2,1024]{1,0:T(2,128)}, u32[]{:S(2)}) copy-start(f32[2,1024]{1,0:T(2,128)} %param.15) | copy-start | bytes 24580
  131.7 5.1 %copy-start.20 = (f32[1024]{0:T(1024)S(1)}, f32[1024]{0:T(1024)}, u32[]{:S(2)}) copy-start(f32[1024]{0:T(1024)} %param.12) | copy-start | bytes 12292
  131.7 5.1 %copy-start.30 = (f32[4]{0:T(128)S(1)}, f32[4]{0:T(128)}, u32[]{:S(2)}) copy-start(f32[4]{0:T(128)} %copy-done.29) | copy-start | bytes 52
  131.7 5.1 %copy-start.32 = (f32[4]{0:T(128)S(1)}, f32[4]{0:T(128)}, u32[]{:S(2)}) copy-start(f32[4]{0:T(128)} %copy-done.31) | copy-start | bytes 52
  131.7 5.2 %copy-start.23 = (f32[24]{0:T(128)S(1)}, f32[24]{0:T(128)}, u32[]{:S(2)}) copy-start(f32[24]{0:T(128)} %copy-done.21) | copy-start | bytes 292
  131.7 5.2 %copy-start.26 = (f32[24]{0:T(128)S(1)}, f32[24]{0:T(128)}, u32[]{:S(2)}) copy-start(f32[24]{0:T(128)} %copy-done.24) | copy-start | bytes 292
  131.8 5.3 %copy-start.7 = (f32[4,24,16,8,8]{1,4,3,2,0:T(8,128)S(1)}, f32[4,24,16,8,8]{1,4,3,2,0:T(8,128)}, u32[]{:S(2)}) copy-start(f32[4,24,16,8,8]{1,4,3,2,0:T(8,128)} %get-tuple-element.10) | copy-start | bytes 1179652
  133.3 17.5 %all-to-all-start.3 = ((f32[8,4,24,128]{3,1,2,0:T(4,128)}), f32[8,4,24,128]{3,1,2,0:T(4,128)S(1)}, u32[]{:S(2)}, u32[]{:S(2)}) async-start(f32[8,4,24,128]{3,1,2,0:T(4,128)} %copy.174), calls=%async_computation.3 | async-start | bytes 786432 | tf_op jit(solution)/shard_map/all_to_all | solution.py:220
  (8 other events, 15.4 us)
where the time goes:
time: 153 us; the launch traced here: 152 us
  local copies, waits for them, and re-layouts  47.4 us (31%)
  other arithmetic  34.7 us (23%)
  starting transfers between devices  24.9 us (16%)
  blocking collectives  21.1 us (14%)
  waiting for transfers between devices  20.1 us (13%)
  matrix products  2.79 us (2%)
    all_to_all x1, blocking collectives, shards(): lax.all_to_all(levels, 'spec', split_axis=2, concat_axis=0, tiled=True)  21.1 us
    all_to_all x1, waiting for transfers between devices, shards(): lax.all_to_all(split_rows, 'spec', split_axis=0, concat_axis=0, tiled=True)  13.1 us
    all_to_all x1, starting transfers between devices, shards(): lax.all_to_all(requests, 'blk', split_axis=0, concat_axis=0, tiled=True)  11 us
    all_to_all x1, starting transfers between devices, shards(): lax.all_to_all(located, 'blk', split_axis=0, concat_axis=0, tiled=True)  10.5 us
    gather x3, local copies, waits for them, and re-layouts, shards(): jnp.take(replies.reshape(peer_count * capacity, -1), remote_index, axis=0)  8.47 us
    convert_element_type x1, other arithmetic, shards(): moved.astype(jnp.bfloat16)  7.67 us
    gather x3, local copies, waits for them, and re-layouts, shards(): local_rows = jnp.take(edge_rows, wanted_ids, axis=0)  7.21 us
    all_to_all x1, waiting for transfers between devices, shards(): lax.all_to_all(located, 'blk', split_axis=0, concat_axis=0, tiled=True)  7 us
  transfers between devices with their start and end apart: 3, of which 2 were waited for; matrix products, arithmetic and copies ran while one was open for 29% of the time, Pallas kernels for 0%

commit v1 on v0

--- a/solution.py
+++ b/solution.py
@@ -210,7 +210,12 @@
         freq_local, angle_count, group_count, point_count // group_count
     )
     result = nonlinear(
-        lax.all_to_all(levels, "spec", split_axis=2, concat_axis=0, tiled=True)[:, :, 0, :],
+        jnp.concatenate(
+            lax.all_to_all(
+                jnp.stack(jnp.split(levels, lax.axis_size("spec"), axis=2)), "spec", 0, 0
+            ),
+            axis=0,
+        )[:, :, 0, :],
         freq_weights,
         angle_weights,
         transfer_rate,

time: 153 us -> 146 us (0.954)
  waiting for transfers between devices: 20.1 us -> 12.7 us
    all_to_all x1, waiting for transfers between devices: 7 us -> 0.01 us  [shards(): lax.all_to_all(located, 'blk', split_axis=0, concat_axis=0, tiled=True)]
    convert_element_type x1 -> x0, local copies, waits for them, and re-layouts: 1.56 us -> none  [shards(): moved.astype(jnp.bfloat16)]
    unnamed x75 -> x70, local copies, waits for them, and re-layouts: 5.03 us -> 5 us
  transfers between devices with their start and end apart: 3 -> 3, of which waited for: 2 -> 1; matrix products, arithmetic and copies ran while one was open for 29% -> 31% of each run, Pallas kernels for 0% -> 0%
where the time goes in v1:
time: 146 us; the launch traced here: 145 us
  local copies, waits for them, and re-layouts  46.9 us (32%)
  other arithmetic  35.8 us (25%)
  starting transfers between devices  24.9 us (17%)
  blocking collectives  20.9 us (14%)
  waiting for transfers between devices  12.7 us (9%)
  matrix products  2.79 us (2%)
    all_to_all x1, blocking collectives, shards(): lax.all_to_all(jnp.stack(jnp.split(levels, lax.axis_size('spec'), axis=2)...  20.9 us
    all_to_all x1, waiting for transfers between devices, shards(): lax.all_to_all(split_rows, 'spec', split_axis=0, concat_axis=0, tiled=True)  12.7 us
    all_to_all x1, starting transfers between devices, shards(): lax.all_to_all(requests, 'blk', split_axis=0, concat_axis=0, tiled=True)  11 us
    all_to_all x1, starting transfers between devices, shards(): lax.all_to_all(located, 'blk', split_axis=0, concat_axis=0, tiled=True)  10.5 us
    gather x3, local copies, waits for them, and re-layouts, shards(): jnp.take(replies.reshape(peer_count * capacity, -1), remote_index, axis=0)  8.47 us
    convert_element_type x1, other arithmetic, shards(): moved.astype(jnp.bfloat16)  7.45 us
    gather x3, local copies, waits for them, and re-layouts, shards(): local_rows = jnp.take(edge_rows, wanted_ids, axis=0)  7.34 us
    unnamed x70, local copies, waits for them, and re-layouts  5 us
  transfers between devices with their start and end apart: 3, of which 1 were waited for; matrix products, arithmetic and copies ran while one was open for 31% of the time, Pallas kernels for 0%

profile of v1, /device:TPU:6, one launch (start us, length us, event | category | flops | bytes accessed | tf_op | source)
XLA Modules:
  0.0 144.9 jit_solution(4871420596746427262)
XLA Ops:
  0.0 1.2 compare_reduce_fusion
  2.9 1.2 compare_and_fusion
  5.0 11.0 %all-to-all-start = ((s32[64,1,2]{2,1,0:T(1,128)}), s32[64,1,2]{2,1,0:T(1,128)}, u32[]{:S(2)}, u32[]{:S(2)}) async-start(s32[64,1,2]{2,1,0:T(1,128)} %copy.170), calls=%async_computation | async-start | bytes 65536 | tf_op jit(solution)/shard_map/all_to_all | solution.py:196
  20.4 1.6 %copy.166 = f32[4,24,1024]{1,2,0:T(8,128)S(1)} copy(f32[4,24,1024]{2,1,0:T(8,128)} %param.11) | data formatting | bytes 786432 | tf_op args[0]
  22.0 1.0 add_multiply_fusion.1
  23.1 1.3 copy-done
  24.4 1.3 slice_multiply_fusion.7
  28.2 1.2 multiply_subtract_fusion.1
  29.4 2.4 %maximum_multiply_fusion.1 = (f32[4,24,16,8,8]{1,4,3,2,0:T(8,128)}, f32[4,24,16,8,8]{1,4,3,2,0:T(8,128)}) fusion(f32[4,24,16,8,8]{1,4,3,2,0:T(8,128)S(1)} %bitcast.156, f32[24,16,8,8]{0,3,2,1:T(8,128)S(1)} %multiply_subtract_fusion.1, f32[4,16,8,8]{3,2,1,0:T(8,128)S(1)} %copy.169), kind=kLoop, calls=%fused_computation.17 | loop fusion | flops 786432 | bytes 1294336 | tf_op jit(solution)/shard_map/mul | solution.py:68
  31.8 1.2 maximum_bitcast_fusion
  33.6 3.2 %copy.173 = f32[16,4,4,24,8]{4,3,2,1,0:T(8,128)} copy(f32[16,4,4,24,8]{3,4,1,0,2:T(8,128)} %maximum_bitcast_fusion) | data formatting | bytes 393216 | tf_op jit(solution)/shard_map/transpose | solution.py:178
  36.8 3.4 %reshape.421 = f32[64,768]{1,0:T(8,128)S(1)} reshape(f32[16,4,4,24,8]{4,3,2,1,0:T(8,128)} %copy.173) | data formatting | bytes 393216 | tf_op jit(solution)/shard_map/reshape | solution.py:178
  41.1 3.7 %slice.162 = f32[4,1,16,8,8]{1,4,3,2,0:T(8,128)} slice(f32[4,24,16,8,8]{1,4,3,2,0:T(8,128)} %get-tuple-element.23), slice={[0:4], [23:24], [0:16], [0:8], [0:8]} | slice | bytes 32768 | tf_op jit(solution)/shard_map/jit(_roll_static)/slice | solution.py:68
  44.8 2.0 %slice.164 = f32[4,23,16,8,8]{1,4,3,2,0:T(8,128)} slice(f32[4,24,16,8,8]{1,4,3,2,0:T(8,128)S(1)} %copy-done.3), slice={[0:4], [1:24], [0:16], [0:8], [0:8]} | slice | bytes 753664 | tf_op jit(solution)/shard_map/jit(_roll_static)/slice | solution.py:68
  48.5 1.6 %gather_fusion = f32[128,768]{1,0:T(8,128)} fusion(f32[64,768]{1,0:T(8,128)S(1)} %reshape.421, s32[1024]{0:T(1024)S(1)} %get-tuple-element.54), kind=kCustom, calls=%fused_computation | custom fusion | bytes 786944 | tf_op jit(solution)/shard_map/jit(_take)/gather | solution.py:195
  50.0 2.0 %reshape.427 = f32[64,2,768]{2,1,0:T(2,128)} reshape(f32[128,768]{1,0:T(8,128)} %gather_fusion) | data formatting | bytes 786432 | tf_op jit(solution)/shard_map/jit(_take)/gather | solution.py:195
  52.1 2.0 %broadcast_select_fusion = f32[64,2,768]{2,1,0:T(2,128)} fusion(f32[64,2,768]{2,1,0:T(2,128)} %reshape.427, pred[64,2]{1,0:T(8,128)(4,1)S(1)} %copy.172), kind=kLoop, calls=%fused_computation.63 | loop fusion | flops 98304 | bytes 786560 | tf_op jit(solution)/shard_map/jit(_take)/select_n | solution.py:195
  54.1 10.5 %all-to-all-start.1 = ((f32[64,2,768]{2,1,0:T(2,128)}), f32[64,2,768]{2,1,0:T(2,128)}, u32[]{:S(2)}, u32[]{:S(2)}) async-start(f32[64,2,768]{2,1,0:T(2,128)} %broadcast_select_fusion), calls=%async_computation.1 | async-start | bytes 786432 | tf_op jit(solution)/shard_map/all_to_all | solution.py:198
  64.6 4.4 %slice_multiply_fusion.3 = (f32[4,24,16,7,8]{1,4,3,2,0:T(8,128)}, f32[4,24,16,7,8]{1,4,3,2,0:T(8,128)}) fusion(f32[4,24,16,8,8]{1,4,3,2,0:T(8,128)S(1)} %bitcast.157, f32[4,24,16,8,8]{1,4,3,2,0:T(8,128)} %copy-done.5), kind=kLoop, calls=%fused_computation.24 | loop fusion | flops 430080 | bytes 2064384 | tf_op jit(solution)/shard_map/mul | solution.py:59
  69.0 2.7 %slice_multiply_fusion.1 = (f32[4,24,16,8,7]{1,4,3,2,0:T(8,128)}, f32[4,24,16,8,7]{1,4,3,2,0:T(8,128)}) fusion(f32[4,24,16,8,8]{1,4,3,2,0:T(8,128)S(1)} %bitcast.158, f32[4,24,16,8,8]{1,4,3,2,0:T(8,128)S(1)} %copy-done.1), kind=kLoop, calls=%fused_computation.12 | loop fusion | flops 430080 | bytes 2064384 | tf_op jit(solution)/shard_map/mul | solution.py:57
  72.6 3.4 %gather.20 = f32[16,4,4,24,8]{4,3,2,1,0:T(8,128)} reshape(f32[64,768]{1,0:T(8,128)S(1)} %gather_fusion.2) | data formatting | bytes 393216 | tf_op jit(solution)/shard_map/jit(_take)/gather | solution.py:201
  75.9 3.2 %copy.177 = f32[16,4,4,24,8]{3,4,1,0,2:T(8,128)} copy(f32[16,4,4,24,8]{4,3,2,1,0:T(8,128)} %gather.20) | data formatting | bytes 393216 | tf_op jit(solution)/shard_map/jit(_take)/gather | solution.py:201
  79.1 1.3 reshape.422
  80.4 1.5 %gather_fusion.1 = f32[64,768]{1,0:T(8,128)} fusion(f32[128,768]{1,0:T(8,128)S(1)} %reshape.422, s32[1024]{0:T(1024)} %pad_clamp_fusion.1), kind=kCustom, calls=%fused_computation.1 | custom fusion | bytes 393472 | tf_op jit(solution)/shard_map/jit(_take)/gather | solution.py:200
  81.8 3.8 %gather.18 = f32[16,4,4,24,8]{4,3,2,1,0:T(8,128)} reshape(f32[64,768]{1,0:T(8,128)} %gather_fusion.1) | data formatting | bytes 393216 | tf_op jit(solution)/shard_map/jit(_take)/gather | solution.py:200
  85.7 3.2 %copy.176 = f32[16,4,4,24,8]{3,4,1,0,2:T(8,128)} copy(f32[16,4,4,24,8]{4,3,2,1,0:T(8,128)} %gather.18) | data formatting | bytes 393216 | tf_op jit(solution)/shard_map/jit(_take)/gather | solution.py:200
  88.8 2.0 %select_bitcast_fusion = f32[4,24,16,4,8]{1,4,3,2,0:T(8,128)S(1)} fusion(f32[16,4,4,24,8]{3,4,1,0,2:T(8,128)} %copy.177, f32[16,4,4,24,8]{3,4,1,0,2:T(8,128)} %copy.176, pred[16,4]{1,0:T(8,128)(4,1)S(1)} %copy-done.22, pred[16,4]{1,0:T(8,128)(4,1)S(1)} %broadcast_in_dim.64, pred[16,4]{1,0:T(8,128)(4,1)S(1)} %broadcast_in_dim.62), kind=kLoop, calls=%fused_computation.41 | loop fusion | flops 147456 | bytes 590016 | tf_op jit(solution)/shard_map/transpose | solution.py:203
  91.2 1.3 copy-done.2
  93.1 7.5 %fusion.97 = (bf16[4,24,16,8,8]{1,4,3,2,0:T(8,128)(2,1)S(1)}, f32[4,24,16,8,8]{1,4,3,2,0:T(8,128)}) fusion(f32[4,24,16,1,8]{1,4,3,2,0:T(8,128)S(1)} %get-tuple-element.34, f32[4,24,16,1,8]{1,4,3,2,0:T(8,128)S(1)} %get-tuple-element.35, f32[4,24,16,8,8]{1,3,2,0,4:T(8,128)S(1)} %pad_add_fusion, f32[4,1,16,8,8]{1,4,3,2,0:T(8,128)S(1)} %bitcast.161, ...), kind=kLoop, calls=%fused_computation.192 | loop fusion | flops 2752512 | bytes 3780800 | tf_op jit(solution)/shard_map/convert_element_type | solution.py:209
  101.6 20.9 %all_to_all.30 = bf16[8,4,24,1,128]{4,2,3,1,0:T(8,128)(2,1)S(1)} all-to-all(bf16[8,4,24,1,128]{4,2,3,1,0:T(8,128)(2,1)S(1)} %constant_dynamic-update-slice_fusion), channel_id=1, replica_groups=mesh['blk'=64,'spec'=8] {'spec'}, dimensions={0} | all-to-all | bytes 393216 | tf_op jit(solution)/shard_map/all_to_all | solution.py:214
  126.7 3.5 %all-to-all-start.3 = ((f32[8,4,24,128]{3,1,2,0:T(4,128)}), f32[8,4,24,128]{3,1,2,0:T(4,128)S(1)}, u32[]{:S(2)}, u32[]{:S(2)}) async-start(f32[8,4,24,128]{3,1,2,0:T(4,128)} %copy.209), calls=%async_computation.3 | async-start | bytes 786432 | tf_op jit(solution)/shard_map/all_to_all | solution.py:225
  131.0 12.7 %all-to-all-done.3 = f32[8,4,24,128]{3,1,2,0:T(4,128)S(1)} async-done(((f32[8,4,24,128]{3,1,2,0:T(4,128)}), f32[8,4,24,128]{3,1,2,0:T(4,128)S(1)}, u32[]{:S(2)}, u32[]{:S(2)}) %all-to-all-start.3) | async-done | bytes 393248 | tf_op jit(solution)/shard_map/all_to_all | solution.py:225
  (141 shorter events, 21.1 us)
Async XLA Ops:
  5.0 41.8 %all-to-all-start = ((s32[64,1,2]{2,1,0:T(1,128)}), s32[64,1,2]{2,1,0:T(1,128)}, u32[]{:S(2)}, u32[]{:S(2)}) async-start(s32[64,1,2]{2,1,0:T(1,128)} %copy.170), calls=%async_computation | async-start | bytes 65536 | tf_op jit(solution)/shard_map/all_to_all | solution.py:196
  16.0 7.0 %copy-start.23 = (f32[4]{0:T(128)}, f32[4]{0:T(128)S(1)}, u32[]{:S(2)}) copy-start(f32[4]{0:T(128)S(1)} %get-tuple-element.49) | copy-start | bytes 52
  16.0 7.0 %copy-start.25 = (f32[4]{0:T(128)}, f32[4]{0:T(128)S(1)}, u32[]{:S(2)}) copy-start(f32[4]{0:T(128)S(1)} %broadcast_multiply_fusion.3) | copy-start | bytes 52
  19.5 3.6 %copy-start.11 = (f32[16,8,8]{2,1,0:T(8,128)}, f32[16,8,8]{2,1,0:T(8,128)S(1)}, u32[]{:S(2)}) copy-start(f32[16,8,8]{2,1,0:T(8,128)S(1)} %add.194) | copy-start | bytes 12292
  19.6 3.5 %copy-start.13 = (f32[16,8,8]{2,1,0:T(8,128)}, f32[16,8,8]{2,1,0:T(8,128)S(1)}, u32[]{:S(2)}) copy-start(f32[16,8,8]{2,1,0:T(8,128)S(1)} %add.197) | copy-start | bytes 12292
  20.4 2.7 %copy-start.15 = (f32[16,8,8]{2,1,0:T(8,128)}, f32[16,8,8]{2,1,0:T(8,128)S(1)}, u32[]{:S(2)}) copy-start(f32[16,8,8]{2,1,0:T(8,128)S(1)} %mul.536) | copy-start | bytes 12292
  23.1 2.6 %copy-start.5 = (f32[4,24,16,8,8]{1,4,3,2,0:T(8,128)}, f32[4,24,16,8,8]{1,4,3,2,0:T(8,128)S(1)}, u32[]{:S(2)}) copy-start(f32[4,24,16,8,8]{1,4,3,2,0:T(8,128)S(1)} %get-tuple-element.38) | copy-start | bytes 1179652
  29.4 2.4 %copy-start.8 = (f32[4,24,16,8,1]{1,4,3,2,0:T(1,128)S(1)}, f32[4,24,16,8,1]{1,4,3,2,0:T(1,128)}, u32[]{:S(2)}) copy-start(f32[4,24,16,8,1]{1,4,3,2,0:T(1,128)} %get-tuple-element.20) | copy-start | bytes 147460
  29.4 2.4 %copy-start.9 = (f32[4,24,16,1,8]{1,4,3,2,0:T(8,128)S(1)}, f32[4,24,16,1,8]{1,4,3,2,0:T(8,128)}, u32[]{:S(2)}) copy-start(f32[4,24,16,1,8]{1,4,3,2,0:T(8,128)} %get-tuple-element.21) | copy-start | bytes 147460
  29.4 2.4 %copy-start.10 = (f32[4,24,16,1,8]{1,4,3,2,0:T(8,128)S(1)}, f32[4,24,16,1,8]{1,4,3,2,0:T(8,128)}, u32[]{:S(2)}) copy-start(f32[4,24,16,1,8]{1,4,3,2,0:T(8,128)} %get-tuple-element.22) | copy-start | bytes 147460
  36.8 3.5 %copy-start.27 = (pred[64]{0:T(512)(128)(4,1)S(1)}, pred[64]{0:T(512)(128)(4,1)}, u32[]{:S(2)}) copy-start(pred[64]{0:T(512)(128)(4,1)} %get-tuple-element.45) | copy-start | bytes 196
  36.8 3.6 %copy-start.29 = (pred[64]{0:T(512)(128)(4,1)S(1)}, pred[64]{0:T(512)(128)(4,1)}, u32[]{:S(2)}) copy-start(pred[64]{0:T(512)(128)(4,1)} %get-tuple-element.13) | copy-start | bytes 196
  41.1 3.7 %copy-start.3 = (f32[4,24,16,8,8]{1,4,3,2,0:T(8,128)S(1)}, f32[4,24,16,8,8]{1,4,3,2,0:T(8,128)}, u32[]{:S(2)}) copy-start(f32[4,24,16,8,8]{1,4,3,2,0:T(8,128)} %get-tuple-element.24) | copy-start | bytes 1179652
  44.8 3.1 %copy-start.30 = (s32[64]{0:T(128)S(1)}, s32[64]{0:T(128)}, u32[]{:S(2)}) copy-start(s32[64]{0:T(128)} %compare_select_fusion.2) | copy-start | bytes 772
  54.1 25.0 %all-to-all-start.1 = ((f32[64,2,768]{2,1,0:T(2,128)}), f32[64,2,768]{2,1,0:T(2,128)}, u32[]{:S(2)}, u32[]{:S(2)}) async-start(f32[64,2,768]{2,1,0:T(2,128)} %broadcast_select_fusion), calls=%async_computation.1 | async-start | bytes 786432 | tf_op jit(solution)/shard_map/all_to_all | solution.py:198
  64.6 4.5 %copy-start.1 = (f32[4,24,16,8,8]{1,4,3,2,0:T(8,128)S(1)}, f32[4,24,16,8,8]{1,4,3,2,0:T(8,128)}, u32[]{:S(2)}) copy-start(f32[4,24,16,8,8]{1,4,3,2,0:T(8,128)} %copy-done) | copy-start | bytes 1179652
  85.7 3.2 %copy-start.22 = (pred[16,4]{1,0:T(8,128)(4,1)S(1)}, pred[16,4]{1,0:T(8,128)(4,1)}, u32[]{:S(2)}) copy-start(pred[16,4]{1,0:T(8,128)(4,1)} %broadcast_in_dim.69) | copy-start | bytes 196
  88.8 2.4 %copy-start.7 = (f32[4,1,16,8,8]{1,4,3,2,0:T(8,128)S(1)}, f32[4,1,16,8,8]{1,4,3,2,0:T(8,128)}, u32[]{:S(2)}) copy-start(f32[4,1,16,8,8]{1,4,3,2,0:T(8,128)} %slice.162) | copy-start | bytes 49156
  90.9 2.3 %copy-start.4 = (f32[4,24,16,8,8]{1,4,3,2,0:T(8,128)S(1)}, f32[4,24,16,8,8]{1,4,3,2,0:T(8,128)}, u32[]{:S(2)}) copy-start(f32[4,24,16,8,8]{1,4,3,2,0:T(8,128)} %get-tuple-element.24) | copy-start | bytes 1179652
  90.9 2.3 %copy-start.12 = (f32[16,8,8]{2,1,0:T(8,128)S(1)}, f32[16,8,8]{2,1,0:T(8,128)}, u32[]{:S(2)}) copy-start(f32[16,8,8]{2,1,0:T(8,128)} %copy-done.11) | copy-start | bytes 12292
  90.9 2.2 %copy-start.14 = (f32[16,8,8]{2,1,0:T(8,128)S(1)}, f32[16,8,8]{2,1,0:T(8,128)}, u32[]{:S(2)}) copy-start(f32[16,8,8]{2,1,0:T(8,128)} %copy-done.13) | copy-start | bytes 12292
  90.9 2.2 %copy-start.16 = (f32[16,8,8]{2,1,0:T(8,128)S(1)}, f32[16,8,8]{2,1,0:T(8,128)}, u32[]{:S(2)}) copy-start(f32[16,8,8]{2,1,0:T(8,128)} %copy-done.15) | copy-start | bytes 12292
  100.6 22.0 %copy-start.18 = (bf16[2,32,32]{2,1,0:T(8,128)(2,1)S(1)}, bf16[2,32,32]{2,1,0:T(8,128)(2,1)}, u32[]{:S(2)}) copy-start(bf16[2,32,32]{2,1,0:T(8,128)(2,1)} %param.19) | copy-start | bytes 12292
  100.6 22.2 %copy-start.17 = (bf16[2,2,24,24]{3,2,1,0:T(8,128)(2,1)S(1)}, bf16[2,2,24,24]{3,2,1,0:T(8,128)(2,1)}, u32[]{:S(2)}) copy-start(bf16[2,2,24,24]{3,2,1,0:T(8,128)(2,1)} %param.20) | copy-start | bytes 13828
  101.5 22.3 %copy-start.28 = (f32[32]{0:T(128)S(1)}, f32[32]{0:T(128)}, u32[]{:S(2)}) copy-start(f32[32]{0:T(128)} %param.21) | copy-start | bytes 388
  125.1 5.0 %copy-start.19 = (s32[1024]{0:T(1024)S(1)}, s32[1024]{0:T(1024)}, u32[]{:S(2)}) copy-start(s32[1024]{0:T(1024)} %param.16) | copy-start | bytes 12292
  125.1 5.0 %copy-start.21 = (f32[2,1024]{1,0:T(2,128)S(1)}, f32[2,1024]{1,0:T(2,128)}, u32[]{:S(2)}) copy-start(f32[2,1024]{1,0:T(2,128)} %param.15) | copy-start | bytes 24580
  125.1 5.1 %copy-start.20 = (f32[1024]{0:T(1024)S(1)}, f32[1024]{0:T(1024)}, u32[]{:S(2)}) copy-start(f32[1024]{0:T(1024)} %param.12) | copy-start | bytes 12292
  125.2 5.1 %copy-start.24 = (f32[4]{0:T(128)S(1)}, f32[4]{0:T(128)}, u32[]{:S(2)}) copy-start(f32[4]{0:T(128)} %copy-done.23) | copy-start | bytes 52
  125.2 5.1 %copy-start.26 = (f32[4]{0:T(128)S(1)}, f32[4]{0:T(128)}, u32[]{:S(2)}) copy-start(f32[4]{0:T(128)} %copy-done.25) | copy-start | bytes 52
  125.2 5.2 %copy-start.6 = (f32[4,24,16,8,8]{1,4,3,2,0:T(8,128)S(1)}, f32[4,24,16,8,8]{1,4,3,2,0:T(8,128)}, u32[]{:S(2)}) copy-start(f32[4,24,16,8,8]{1,4,3,2,0:T(8,128)} %get-tuple-element.10) | copy-start | bytes 1179652
  126.7 17.0 %all-to-all-start.3 = ((f32[8,4,24,128]{3,1,2,0:T(4,128)}), f32[8,4,24,128]{3,1,2,0:T(4,128)S(1)}, u32[]{:S(2)}, u32[]{:S(2)}) async-start(f32[8,4,24,128]{3,1,2,0:T(4,128)} %copy.209), calls=%async_computation.3 | async-start | bytes 786432 | tf_op jit(solution)/shard_map/all_to_all | solution.py:225
  (2 other events, 2.9 us)
